TPU v7x, 32 devices: a whole 2x2x4 slice. The times are simulated.
32 devices in a mesh: dp: 8 (over z, x), mp: 4 (over y, core).
Axes of the slice: x: 2, y: 2, z: 4, core: 2. Of those that a mesh axis runs over, the one named last changes fastest.
Arguments:
- tokens: bfloat16 [16384, 768], P('dp'), may hold values from -6 to 6
- cotangent: bfloat16 [16384, 768], P('dp'), may hold values from -6 to 6
- qkv_weight: bfloat16 [3, 768, 768], P(None, None, 'mp'), may hold values from -0.21875 to 0.21875
- col_bias: bfloat16 [2, 768], P(None, 'mp'), may hold values from -3 to 3
- out_weight: bfloat16 [768, 768], P('mp'), may hold values from -1.75 to 1.75
- in_weight: bfloat16 [768, 3072], P(None, 'mp'), may hold values from -0.21875 to 0.21875
- in_bias: bfloat16 [3072], P('mp'), may hold values from -3 to 3
- down_weight: bfloat16 [3072, 768], P('mp'), may hold values from -0.109375 to 0.109375
- vectors: bfloat16 [6, 768], replicated, may hold values from 0.5 to 1.5
- slot_is_long: int32 [32], P('dp'), may hold values from 0 to 1
- seq_len: int32 [32, 4], P('dp'), may hold values from 1 to 128, as said below
- master: float32 [4, 8, 221472], P('mp', 'dp'), may hold values from -0.18 to 0.18
- first_moment: float32 [4, 8, 221472], P('mp', 'dp'), as said below
- second_moment: float32 [4, 8, 221472], P('mp', 'dp'), as said below
- average: float32 [4, 8, 221472], P('mp', 'dp'), may hold values from -0.18 to 0.18
Outputs:
- output: bfloat16 [16384, 768], P('dp')
- grad_input: float32 [16384, 768], P('dp')
- vector_grad: float32 [4, 8, 144], P('mp', 'dp')
- new_master: float32 [4, 8, 221472], P('mp', 'dp')
- new_first: float32 [4, 8, 221472], P('mp', 'dp')
- new_second: float32 [4, 8, 221472], P('mp', 'dp')
- new_average: float32 [4, 8, 221472], P('mp', 'dp')
Inputs may be any that keep to these rules, and one draw needn't show every extreme that they name: `seq_len`: in every slot one of the four entries equals 128. `first_moment`: entries of both signs, none near zero. `second_moment`: every entry positive.
All inputs are finite; a program needn't handle non-finite values.
Results may differ from a plain program's by a relative error of at most 0.02.
Values may be sent and summed in bfloat16 or wider, within the bound.
No kernel may reach another device: no remote copies, remote signals or barrier semaphores. Data moves between devices by JAX's collectives and lax.ppermute only.
A program may use at most 128 MiB of HBM per device.

v0:
```python
import jax
import jax.numpy as jnp
from jax import lax
from jax.sharding import PartitionSpec as P

HDIM = 64
SLOT_TOKENS = 512
SHORT_TOKENS = 128
STEP = 3
NORM_EPS = 1e-12


def slot_masks(kind, sequence_lengths):
    pos = jnp.arange(SLOT_TOKENS, dtype=jnp.int32)
    block = pos // SHORT_TOKENS
    is_long = kind == 1
    segment = jnp.where(is_long, 0, block)
    inner = jnp.where(is_long, pos, pos % SHORT_TOKENS)
    picks = block[:, None] == jnp.arange(sequence_lengths.shape[0], dtype=jnp.int32)[None, :]
    short_len = jnp.sum(jnp.where(picks, sequence_lengths[None, :], 0), axis=1)
    seg_len = jnp.where(is_long, jnp.sum(sequence_lengths), short_len)
    valid = inner < seg_len
    allowed = (segment[:, None] == segment[None, :]) & valid[None, :]
    key_ok = jnp.arange(SHORT_TOKENS, dtype=jnp.int32)[None, :] < sequence_lengths[:, None]
    return (allowed, valid, key_ok)


def layer_norm(z, gain, shift):
    centered = z - jnp.mean(z, axis=-1, keepdims=True)
    var = jnp.mean(centered * centered, axis=-1, keepdims=True)
    return centered * lax.rsqrt(var + NORM_EPS) * gain + shift


def gelu_exact(u):
    return 0.5 * u * (1.0 + jax.scipy.special.erf(u * 2.0 ** (-0.5)))


def block_scores(query, keys, mask):
    scores = jnp.einsum("bqhe,bkhe->bhqk", query, keys, preferred_element_type=jnp.float32)
    return jnp.where(mask[:, None], scores, -1000000000.0)


def attend_blocks(query, keys, values, mask):
    scores = block_scores(query, keys, mask)
    top = jnp.max(scores, axis=-1, keepdims=True)
    expd = jnp.exp(scores - top)
    total = jnp.sum(expd, axis=-1, keepdims=True)
    probs = expd / total
    lse = top[..., 0] + jnp.log(total[..., 0])
    context = jnp.einsum(
        "bhqk,bkhe->bqhe", probs.astype(jnp.bfloat16), values, preferred_element_type=jnp.float32
    )
    return (context, lse)


def attend_back(query, keys, values, dctx, lse, mask):
    scores = block_scores(query, keys, mask)
    probs = jnp.where(mask[:, None], jnp.exp(scores - lse[..., None]), 0.0)
    dprob = jnp.einsum("bqhe,bkhe->bhqk", dctx, values, preferred_element_type=jnp.float32)
    dscore = probs * (dprob - jnp.sum(probs * dprob, axis=-1, keepdims=True))
    dscore_b = dscore.astype(jnp.bfloat16)
    d_query = jnp.einsum("bhqk,bkhe->bqhe", dscore_b, keys, preferred_element_type=jnp.float32)
    d_keys = jnp.einsum("bhqk,bqhe->bkhe", dscore_b, query, preferred_element_type=jnp.float32)
    d_values = jnp.einsum(
        "bhqk,bqhe->bkhe", probs.astype(jnp.bfloat16), dctx, preferred_element_type=jnp.float32
    )
    return (
        d_query.astype(jnp.bfloat16),
        d_keys.astype(jnp.bfloat16),
        d_values.astype(jnp.bfloat16),
    )


def slot_forward(item):
    query, keys, values, kind, sequence_lengths = item
    allowed, valid, key_ok = slot_masks(kind, sequence_lengths)

    def whole():
        context, lse = attend_blocks(query[None], keys[None], values[None], allowed[None])
        return (context[0], lse[0])

    return whole()


def slot_backward(item):
    query, keys, values, dctx, lse, kind, sequence_lengths = item
    allowed, valid, key_ok = slot_masks(kind, sequence_lengths)

    def whole():
        grads = attend_back(
            query[None], keys[None], values[None], dctx[None], lse[None], allowed[None]
        )
        return tuple((g[0] for g in grads))

    return whole()


def body(
    tokens,
    cotangent,
    qkv_weight,
    col_bias,
    out_weight,
    in_weight,
    in_bias,
    down_weight,
    vectors,
    slot_is_long,
    seq_len,
    master,
    first_moment,
    second_moment,
    average,
):
    rows = tokens.shape[0]
    slots = slot_is_long.shape[0]
    heads_here = qkv_weight.shape[2] // HDIM
    scale = HDIM ** (-0.5)
    ndata = lax.axis_size("dp")
    nmodel = lax.axis_size("mp")
    vec = vectors.astype(jnp.float32)
    bias = col_bias.astype(jnp.float32)
    proj = jnp.einsum("td,cde->cte", tokens, qkv_weight, preferred_element_type=jnp.float32)
    query = ((proj[0] + bias[0]) * scale).astype(jnp.bfloat16)
    keys = proj[1].astype(jnp.bfloat16)
    values = (proj[2] + bias[1]).astype(jnp.bfloat16)
    shape4 = (slots, SLOT_TOKENS, heads_here, HDIM)
    query4 = query.reshape(shape4)
    keys4 = keys.reshape(shape4)
    values4 = values.reshape(shape4)
    context, lse = lax.map(slot_forward, (query4, keys4, values4, slot_is_long, seq_len))
    context_b = context.reshape(rows, -1).astype(jnp.bfloat16)
    attn_part = jnp.dot(context_b, out_weight, preferred_element_type=jnp.float32).astype(
        jnp.bfloat16
    )
    attn = lax.psum(attn_part, "mp").astype(jnp.float32)
    z_one = tokens.astype(jnp.float32) + attn + vec[4]
    x_one, norm_one_pull = jax.vjp(layer_norm, z_one, vec[0], vec[1])
    x_one_b = x_one.astype(jnp.bfloat16)
    pre = jnp.dot(x_one_b, in_weight, preferred_element_type=jnp.float32) + in_bias.astype(
        jnp.float32
    )
    hidden, gelu_pull = jax.vjp(gelu_exact, pre)
    hidden_b = hidden.astype(jnp.bfloat16)
    down_part = jnp.dot(hidden_b, down_weight, preferred_element_type=jnp.float32).astype(
        jnp.bfloat16
    )
    ffn = lax.psum(down_part, "mp").astype(jnp.float32)
    z_two = x_one + ffn + vec[5]
    output, norm_two_pull = jax.vjp(layer_norm, z_two, vec[2], vec[3])
    valid = jax.vmap(lambda kk, ll: slot_masks(kk, ll)[1])(slot_is_long, seq_len).reshape(rows)
    grad_out = cotangent.astype(jnp.float32) * valid[:, None].astype(jnp.float32)
    dz_two, d_gain_two, d_shift_two = norm_two_pull(grad_out)
    d_bias_two = jnp.sum(dz_two, axis=0)
    dz_two_b = dz_two.astype(jnp.bfloat16)
    g_down = jnp.dot(hidden_b.T, dz_two_b, preferred_element_type=jnp.float32)
    d_hidden = jnp.dot(dz_two_b, down_weight.T, preferred_element_type=jnp.float32)
    d_pre = gelu_pull(d_hidden)[0]
    d_pre_b = d_pre.astype(jnp.bfloat16)
    g_in = jnp.dot(x_one_b.T, d_pre_b, preferred_element_type=jnp.float32)
    g_inb = jnp.sum(d_pre_b.astype(jnp.float32), axis=0)
    ffn_pieces = (g_in.reshape(ndata, -1), g_down.reshape(ndata, -1), g_inb.reshape(ndata, -1))
    back_one = jnp.dot(d_pre_b, in_weight.T, preferred_element_type=jnp.float32).astype(
        jnp.bfloat16
    )
    dx_one = dz_two + lax.psum(back_one, "mp").astype(jnp.float32)
    dz_one, d_gain_one, d_shift_one = norm_one_pull(dx_one)
    d_bias_out = jnp.sum(dz_one, axis=0)
    dz_one_b = dz_one.astype(jnp.bfloat16)
    g_out = jnp.dot(context_b.T, dz_one_b, preferred_element_type=jnp.float32)
    d_context = jnp.dot(dz_one_b, out_weight.T, preferred_element_type=jnp.float32).astype(
        jnp.bfloat16
    )
    d_query, d_keys, d_values = lax.map(
        slot_backward,
        (query4, keys4, values4, d_context.reshape(shape4), lse, slot_is_long, seq_len),
    )
    d_query = d_query.reshape(rows, -1)
    d_keys = d_keys.reshape(rows, -1)
    d_values = d_values.reshape(rows, -1)
    d_proj = jnp.stack([d_query, d_keys, d_values])
    factors = jnp.array([scale, 1.0, 1.0], jnp.float32)[:, None, None]
    g_qkv = jnp.einsum("td,cte->cde", tokens, d_proj, preferred_element_type=jnp.float32) * factors
    g_col = jnp.stack(
        [
            jnp.sum(d_query.astype(jnp.float32), axis=0) * scale,
            jnp.sum(d_values.astype(jnp.float32), axis=0),
        ]
    )
    back_zero = (
        jnp.dot(d_query, qkv_weight[0].T, preferred_element_type=jnp.float32) * scale
        + jnp.dot(d_keys, qkv_weight[1].T, preferred_element_type=jnp.float32)
        + jnp.dot(d_values, qkv_weight[2].T, preferred_element_type=jnp.float32)
    ).astype(jnp.bfloat16)
    grad_input = dz_one + lax.psum(back_zero, "mp").astype(jnp.float32)
    g_vec = jnp.stack(
        [d_gain_one, d_shift_one, d_gain_two, d_shift_two, d_bias_out, d_bias_two]
    ).reshape(-1)
    share = g_vec.shape[0] // nmodel
    g_vec_mine = lax.dynamic_slice_in_dim(g_vec, lax.axis_index("mp") * share, share)
    attn_pieces = (
        g_qkv.reshape(ndata, -1),
        g_out.reshape(ndata, -1),
        g_col.reshape(ndata, -1),
        g_vec_mine.reshape(ndata, -1),
    )
    summed = (
        lax.psum_scatter(attn_pieces[0], "dp", scatter_dimension=0, tiled=True),
        lax.psum_scatter(attn_pieces[1], "dp", scatter_dimension=0, tiled=True),
        lax.psum_scatter(ffn_pieces[0], "dp", scatter_dimension=0, tiled=True),
        lax.psum_scatter(ffn_pieces[1], "dp", scatter_dimension=0, tiled=True),
        lax.psum_scatter(attn_pieces[2], "dp", scatter_dimension=0, tiled=True),
        lax.psum_scatter(ffn_pieces[2], "dp", scatter_dimension=0, tiled=True),
        lax.psum_scatter(attn_pieces[3], "dp", scatter_dimension=0, tiled=True),
    )
    grad = (jnp.concatenate(summed, axis=1) / ndata).reshape(master.shape)
    vector_grad = (summed[6] / ndata).reshape(1, 1, -1)
    new_first = 0.5 * first_moment + 0.5 * grad
    new_second = 0.5 * second_moment + 0.5 * grad * grad
    corr = 1.0 - 0.5**STEP
    new_master = master - 0.02 * (
        new_first / corr / (jnp.sqrt(new_second / corr) + 1e-08) + 0.01 * master
    )
    new_average = 0.75 * average + 0.25 * new_master
    return (
        output.astype(jnp.bfloat16),
        grad_input,
        vector_grad,
        new_master,
        new_first,
        new_second,
        new_average,
    )


def solution(mesh):
    placed = (
        P("dp", None),
        P("dp", None),
        P(None, None, "mp"),
        P(None, "mp"),
        P("mp", None),
        P(None, "mp"),
        P("mp"),
        P("mp", None),
        P(),
        P("dp"),
        P("dp", None),
        P("mp", "dp", None),
        P("mp", "dp", None),
        P("mp", "dp", None),
        P("mp", "dp", None),
    )
    return jax.shard_map(
        body,
        mesh=mesh,
        in_specs=placed,
        out_specs=(
            P("dp", None),
            P("dp", None),
            P("mp", "dp", None),
            P("mp", "dp", None),
            P("mp", "dp", None),
            P("mp", "dp", None),
            P("mp", "dp", None),
        ),
        check_vma=False,
    )
```

profile of v0, /device:TPU:0, one launch (start us, length us, event | category | flops | bytes accessed | tf_op | source)
XLA Modules:
  0.0 723.3 jit_solution(13496758862264162872)
XLA Ops:
  7.2 4.3 convolution_bitcast_fusion
  22.3 28.6 %while.30 = (s32[]{:T(128)}, bf16[4,512,3,64]{1,3,2,0:T(8,128)(2,1)}, f32[4,3,512]{2,1,0:T(4,128)}, bf16[4,512,3,64]{1,3,2,0:T(8,128)(2,1)S(1)}, s32[4]{0:T(128)...) while((s32[]{:T(128)}, ...), condition=%wide.region_5.6_spmd, body=%wide.region_0.5_spmd.sunk | while | flops 208942080 | bytes 11540152 | solution.py:131
  58.3 69.8 %all-reduce.15.cloned.1.call-done = bf16[2048,768]{1,0:T(8,128)(2,1)} async-done(((bf16[2048,768]{1,0:T(8,128)(2,1)}), bf16[2048,768]{1,0:T(8,128)(2,1)}) %all-reduce.15.cloned.1.call-update) | async-done | bytes 3145744 | tf_op jit(solution)/shard_map/psum | solution.py:136
  128.2 4.1 fusion.74
  135.3 6.7 multiply_convert_fusion.1
  143.6 3.9 convolution_convert_fusion.3
  151.7 64.5 %all-reduce.17.cloned.1.call-done = bf16[2048,768]{1,0:T(8,128)(2,1)} async-done(((bf16[2048,768]{1,0:T(8,128)(2,1)}), bf16[2048,768]{1,0:T(8,128)(2,1)}) %all-reduce.17.cloned.1.call-update) | async-done | bytes 3145744 | tf_op jit(solution)/shard_map/psum | solution.py:148
  216.3 5.4 fusion.126
  227.3 4.7 fusion.125
  232.1 6.4 convert_reduce_fusion
  240.1 4.0 convolution_convert_fusion.2
  244.6 7.9 %fusion.114 = f32[768,768]{1,0:T(8,128)} fusion(bf16[2048,768]{1,0:T(8,128)(2,1)} %copy-done.45, f32[2048,768]{1,0:T(8,128)} %copy-done.7, f32[2048]{0:T(1024)} %copy-done.21), kind=kOutput, calls=%fused_computation.207 | convolution fusion | flops 2419064832 | bytes 11804672 | tf_op jit(solution)/shard_map/dot_general | solution.py:156
  256.0 56.8 %all-reduce.19.cloned.1.call-done = bf16[2048,768]{1,0:T(8,128)(2,1)} async-done(((bf16[2048,768]{1,0:T(8,128)(2,1)}), bf16[2048,768]{1,0:T(8,128)(2,1)}) %all-reduce.19.cloned.1.call-update) | async-done | bytes 3145744 | tf_op jit(solution)/shard_map/psum | solution.py:166
  312.8 9.4 %multiply_reduce_fusion.2 = (f32[768]{0:T(1024)S(1)}, f32[2048]{0:T(1024)S(1)}, f32[768]{0:T(1024)S(1)}, f32[768]{0:T(1024)S(1)}) fusion(f32[2048]{0:T(1024)S(1)} %copy-done.18, bf16[2048,768]{1,0:T(8,128)(2,1)} %all-reduce.19.cloned.1.call-done, f32[2048,768]{1,0:T(8,128)} %copy-done.7, f32[2048]{0:T(1024)S(1)} %copy-done.22, ...), kind=kLoop, calls=%fused_computation.97 | loop fusion | flops 25161472 | bytes 15776768 | tf_op jit(solution)/shard_map/transpose(jvp())/reduce_sum | solution.py:31
  322.3 6.0 fusion.124
  335.1 46.2 %while.31 = (s32[]{:T(128)}, bf16[4,512,3,64]{1,3,2,0:T(8,128)(2,1)}, bf16[4,512,3,64]{1,3,2,0:T(8,128)(2,1)}, bf16[4,512,3,64]{1,3,2,0:T(8,128)(2,1)}, bf16[4,5...) while((s32[]{:T(128)}, ...), condition=%wide.region_23.24_spmd, body=%wide.region_19.23_spmd.sunk | while | flops 511226880 | bytes 26134740 | solution.py:174
  392.3 8.5 %fusion.117 = f32[768,768]{1,0:T(8,128)} fusion(bf16[2048,768]{1,0:T(8,128)(2,1)} %copy-done.44, f32[768]{0:T(1024)S(1)} %copy-done.30, f32[768]{0:T(1024)S(1)} %get-tuple-element.346, f32[2048]{0:T(1024)S(1)} %copy-done.18, bf16[2048,768]{1,0:T(8,128)(2,1)} %all-reduce.15.cloned.1.call-done, bf16[2048,768]{1,0:T(8,128)(2,1)} %param.20, ...), kind=kOutput, calls=%fused_computation.210 | convolution fusion | flops 2430074880 | bytes 11822080 | tf_op jit(solution)/shard_map/dot_general | solution.py:160
  408.7 3.9 fusion.116
  413.6 5.4 multiply_bitcast_fusion
  425.7 35.2 %all-reduce.21.cloned.1.call-done = bf16[2048,768]{1,0:T(8,128)(2,1)} async-done(((bf16[2048,768]{1,0:T(8,128)(2,1)}), bf16[2048,768]{1,0:T(8,128)(2,1)}) %all-reduce.21.cloned.1.call-update) | async-done | bytes 3145744 | tf_op jit(solution)/shard_map/psum | solution.py:195
  460.9 6.0 add_reduce_fusion
  467.1 39.8 %all-reduce.7 = (f32[8,144]{1,0:T(8,128)S(1)}, f32[8,48]{1,0:T(8,128)S(1)}, f32[8,96]{1,0:T(8,128)S(1)}) all-reduce(f32[8,144]{1,0:T(8,128)S(1)} %reshape.865, f32[8,48]{1,0:T(8,128)S(1)} %reshape.871, f32[8,96]{1,0:T(8,128)S(1)} %reshape.872), channel_id=2, replica_groups=mesh['dp'=8,'mp'=4] {'dp'}, use_global_device_ids=true, to_apply=%region_31.32.clone | all-reduce | flops 2304 | bytes 18432
  509.4 188.2 %all-reduce.23.cloned.1.call-done = (f32[8,55296]{1,0:T(8,128)}, f32[8,18432]{1,0:T(8,128)}, f32[8,73728]{1,0:T(8,128)}, f32[8,73728]{1,0:T(8,128)}) async-done(((f32[8,55296]{1,0:T(8,128)}, f32[8,18432]{1,0:T(8,128)}, f32[8,73728]{1,0:T(8,128)}, f32[8,73728]{1,0:T(8,128)}), (f32[8,55296]{1,0:T(8,128)}, f32[8,18432]{1,0:T(8,128)}, f32[8,73728]{1,0:T(8,128)}, ...) | async-done | bytes 7077904
  707.4 9.2 %multiply_add_fusion.1 = (f32[1,1,221472]{2,1,0:T(1,128)}, f32[1,1,221472]{2,1,0:T(1,128)}, f32[1,1,221472]{2,1,0:T(1,128)}, f32[1,1,221472]{2,1,0:T(1,128)}) fusion(f32[1,1,221472]{2,1,0:T(1,128)S(1)} %copy-done.13, f32[1,1,221472]{2,1,0:T(1,128)} %param.31, f32[1,1,221472]{2,1,0:T(1,128)S(1)} %dynamic-update-slice.6, f32[1,1,221472]{2,1,0:T(1,128)} %param.32, ...), kind=kLoop, calls=%fused_computation.144 | loop fusion | flops 3986496 | bytes 7972992 | tf_op jit(solution)/shard_map/add | solution.py:224
  (289 shorter events, 152.8 us)
Async XLA Ops:
  7.2 128.1 %copy-start = (bf16[768,768]{1,0:T(8,128)(2,1)S(1)}, bf16[768,768]{1,0:T(8,128)(2,1)}, u32[]{:S(2)}) copy-start(bf16[768,768]{1,0:T(8,128)(2,1)} %param.25) | copy-start | bytes 3538948
  7.2 121.0 %all-reduce.15.cloned.1.call-start = ((), (), s32[]{:S(2)}) async-start(), calls=%async_computation | async-start | bytes 6291456 | tf_op jit(solution)/shard_map/psum | solution.py:136
  11.5 6.9 copy-start.37
  56.9 159.4 %all-reduce.17.cloned.1.call-start = ((), (), s32[]{:S(2)}) async-start(), calls=%async_computation.1 | async-start | bytes 6291456 | tf_op jit(solution)/shard_map/psum | solution.py:148
  128.2 7.1 copy-start.29
  128.2 7.1 copy-start.33
  135.3 8.4 %copy-start.38 = (bf16[768,768]{1,0:T(8,128)(2,1)S(1)}, bf16[768,768]{1,0:T(8,128)(2,1)}, u32[]{:S(2)}) copy-start(bf16[768,768]{1,0:T(8,128)(2,1)} %param.27) | copy-start | bytes 3538948
  147.6 165.2 %all-reduce.19.cloned.1.call-start = ((), (), s32[]{:S(2)}) async-start(), calls=%async_computation.2 | async-start | bytes 6291456 | tf_op jit(solution)/shard_map/psum | solution.py:166
  223.6 8.4 %slice-start = ((s8[6291456]{0:T(1024)(128)(4,1)}), s8[4194304]{0:T(1024)(128)(4,1)S(1)}, s32[]{:S(2)}) async-start(s8[6291456]{0:T(1024)(128)(4,1)} %bitcast.220), calls=%async_computation.5 | async-start | bytes 8388608
  244.1 216.8 %all-reduce.21.cloned.1.call-start = ((), (), s32[]{:S(2)}) async-start(), calls=%async_computation.3 | async-start | bytes 6291456 | tf_op jit(solution)/shard_map/psum | solution.py:195
  244.6 68.2 %copy-start.18 = (f32[2048]{0:T(1024)S(1)}, f32[2048]{0:T(1024)}, u32[]{:S(2)}) copy-start(f32[2048]{0:T(1024)} %copy-done.17) | copy-start | bytes 24580
  244.6 68.2 %copy-start.22 = (f32[2048]{0:T(1024)S(1)}, f32[2048]{0:T(1024)}, u32[]{:S(2)}) copy-start(f32[2048]{0:T(1024)} %copy-done.21) | copy-start | bytes 24580
  256.0 66.2 %copy-start.25 = (f32[2048]{0:T(1024)S(1)}, f32[2048]{0:T(1024)}, u32[]{:S(2)}) copy-start(f32[2048]{0:T(1024)} %copy-done.24) | copy-start | bytes 24580
  312.8 9.4 %copy-start.4 = (bf16[2048,768]{1,0:T(8,128)(2,1)S(1)}, bf16[2048,768]{1,0:T(8,128)(2,1)}, u32[]{:S(2)}) copy-start(bf16[2048,768]{1,0:T(8,128)(2,1)} %param.20) | copy-start | bytes 9437188
  312.8 9.4 %copy-start.6 = (bf16[2048,768]{1,0:T(8,128)(2,1)S(1)}, bf16[2048,768]{1,0:T(8,128)(2,1)}, u32[]{:S(2)}) copy-start(bf16[2048,768]{1,0:T(8,128)(2,1)} %all-reduce.15.cloned.1.call-done) | copy-start | bytes 9437188
  312.8 9.4 %copy-start.8 = (bf16[2048,768]{1,0:T(8,128)(2,1)S(1)}, bf16[2048,768]{1,0:T(8,128)(2,1)}, u32[]{:S(2)}) copy-start(bf16[2048,768]{1,0:T(8,128)(2,1)} %all-reduce.19.cloned.1.call-done) | copy-start | bytes 9437188
  322.3 8.8 %copy-start.12 = (bf16[192,768]{1,0:T(8,128)(2,1)S(1)}, bf16[192,768]{1,0:T(8,128)(2,1)}, u32[]{:S(2)}) copy-start(bf16[192,768]{1,0:T(8,128)(2,1)} %param.24) | copy-start | bytes 884740
  328.3 6.8 copy-start.41
  328.4 80.3 %copy-start.19 = (f32[2048]{0:T(1024)}, f32[2048]{0:T(1024)S(1)}, u32[]{:S(2)}) copy-start(f32[2048]{0:T(1024)S(1)} %negate_multiply_fusion) | copy-start | bytes 24580
  392.2 305.4 %all-reduce.23.cloned.1.call-start = ((), (), s32[]{:S(2)}) async-start(), calls=%async_computation.4 | async-start | bytes 14155776
  405.8 7.8 %copy-start.43 = (f32[3]{0:T(128)S(1)}, f32[3]{0:T(128)}, u32[]{:S(2)}) copy-start(f32[3]{0:T(128)} %constant.258.clone) | copy-start | bytes 40
  421.0 39.9 %copy-start.20 = (f32[2048]{0:T(1024)S(1)}, f32[2048]{0:T(1024)}, u32[]{:S(2)}) copy-start(f32[2048]{0:T(1024)} %copy-done.19) | copy-start | bytes 24580
  425.7 281.7 %copy-start.13 = (f32[1,1,221472]{2,1,0:T(1,128)S(1)}, f32[1,1,221472]{2,1,0:T(1,128)}, u32[]{:S(2)}) copy-start(f32[1,1,221472]{2,1,0:T(1,128)} %param.34) | copy-start | bytes 2657668
  460.9 255.6 %copy-start.1 = (bf16[768,768]{1,0:T(8,128)(2,1)S(1)}, bf16[768,768]{1,0:T(8,128)(2,1)}, u32[]{:S(2)}) copy-start(bf16[768,768]{1,0:T(8,128)(2,1)} %param.25) | copy-start | bytes 3538948
  (29 other events, 109.3 us)
Sparse Core Ops, SparseCore 0:
  57.0 71.1 all-reduce.14
  147.7 68.5 all-reduce.16
  244.2 68.5 all-reduce.18
  392.3 68.5 all-reduce.20
  465.2 232.3 all-reduce.22
where the time goes:
time: 732 us; the launch traced here: 723 us
  waiting for transfers between devices  415 us (57%)
  matrix products  96 us (13%)
  other arithmetic  87.5 us (12%)
  local copies, waits for them, and re-layouts  64.3 us (9%)
  blocking collectives  39.8 us (5%)
  between operations  14.8 us (2%)
    unnamed x6, waiting for transfers between devices  188 us
    psum x1, waiting for transfers between devices, body(): attn = lax.psum(attn_part, 'mp').astype(jnp.float32)  69.8 us
    psum x1, waiting for transfers between devices, body(): ffn = lax.psum(down_part, 'mp').astype(jnp.float32)  64.5 us
    psum x1, waiting for transfers between devices, body(): dx_one = dz_two + lax.psum(back_one, 'mp').astype(jnp.float32)  56.8 us
    unnamed x1, blocking collectives  39.8 us
    psum x1, waiting for transfers between devices, body(): grad_input = dz_one + lax.psum(back_zero, 'mp').astype(jnp.float32)  35.2 us
    reduce_sum x4, other arithmetic, layer_norm(): centered = z - jnp.mean(z, axis=-1, keepdims=True)  20.3 us
    unnamed x108, local copies, waits for them, and re-layouts  19.8 us
  transfers between devices with their start and end apart: 5, of which 5 were waited for; matrix products, arithmetic and copies ran while one was open for 8% of the time, Pallas kernels for 0%

commit v1 on v0

--- a/solution.py
+++ b/solution.py
@@ -192,7 +192,7 @@
         + jnp.dot(d_keys, qkv_weight[1].T, preferred_element_type=jnp.float32)
         + jnp.dot(d_values, qkv_weight[2].T, preferred_element_type=jnp.float32)
     ).astype(jnp.bfloat16)
-    grad_input = dz_one + lax.psum(back_zero, "mp").astype(jnp.float32)
+    grad_input = dz_one + jnp.sum(lax.all_gather(back_zero, "mp"), axis=0).astype(jnp.float32)
     g_vec = jnp.stack(
         [d_gain_one, d_shift_one, d_gain_two, d_shift_two, d_bias_out, d_bias_two]
     ).reshape(-1)

time: 732 us -> 794 us (1.085)
  waiting for transfers between devices: 415 us -> 475 us
  other arithmetic: 87.5 us -> 96.7 us
    all_gather x0 -> x1, waiting for transfers between devices: none -> 73.5 us  [body(): lax.all_gather(back_zero, 'mp')]
    psum x1 -> x0, waiting for transfers between devices: 35.2 us -> none  [body(): grad_input = dz_one + lax.psum(back_zero, 'mp').astype(jnp.float32)]
    unnamed x6, waiting for transfers between devices: 188 us -> 222 us
    psum x1, waiting for transfers between devices: 56.8 us -> 44.7 us  [body(): dx_one = dz_two + lax.psum(back_one, 'mp').astype(jnp.float32)]
    reduce_sum x0 -> x1, other arithmetic: none -> 8.97 us  [body(): jnp.sum(lax.all_gather(back_zero, 'mp'), axis=0).astype(jnp.float32)]
    unnamed x108 -> x114, local copies, waits for them, and re-layouts: 19.8 us -> 17.6 us
  transfers between devices with their start and end apart: 5 -> 5, of which waited for: 5 -> 5; matrix products, arithmetic and copies ran while one was open for 8% -> 6% of each run, Pallas kernels for 0% -> 0%
where the time goes in v1:
time: 794 us; the launch traced here: 785 us
  waiting for transfers between devices  475 us (60%)
  other arithmetic  96.7 us (12%)
  matrix products  93.1 us (12%)
  local copies, waits for them, and re-layouts  61.8 us (8%)
  blocking collectives  37.5 us (5%)
  between operations  15 us (2%)
    unnamed x6, waiting for transfers between devices  222 us
    all_gather x1, waiting for transfers between devices, body(): lax.all_gather(back_zero, 'mp')  73.5 us
    psum x1, waiting for transfers between devices, body(): attn = lax.psum(attn_part, 'mp').astype(jnp.float32)  69.8 us
    psum x1, waiting for transfers between devices, body(): ffn = lax.psum(down_part, 'mp').astype(jnp.float32)  64.5 us
    psum x1, waiting for transfers between devices, body(): dx_one = dz_two + lax.psum(back_one, 'mp').astype(jnp.float32)  44.7 us
    unnamed x1, blocking collectives  37.5 us
    reduce_sum x4, other arithmetic, layer_norm(): centered = z - jnp.mean(z, axis=-1, keepdims=True)  20.2 us
    unnamed x114, local copies, waits for them, and re-layouts  17.6 us
  transfers between devices with their start and end apart: 5, of which 5 were waited for; matrix products, arithmetic and copies ran while one was open for 6% of the time, Pallas kernels for 0%

profile of v1, /device:TPU:0, one launch (start us, length us, event | category | flops | bytes accessed | tf_op | source)
XLA Modules:
  0.0 785.5 jit_solution(9939046409115414909)
XLA Ops:
  7.2 4.3 convolution_bitcast_fusion
  22.3 28.6 %while.30 = (s32[]{:T(128)}, bf16[4,512,3,64]{1,3,2,0:T(8,128)(2,1)}, f32[4,3,512]{2,1,0:T(4,128)}, bf16[4,512,3,64]{1,3,2,0:T(8,128)(2,1)S(1)}, s32[4]{0:T(128)...) while((s32[]{:T(128)}, ...), condition=%wide.region_5.6_spmd, body=%wide.region_0.5_spmd.sunk | while | flops 208942080 | bytes 11540152 | solution.py:131
  58.4 69.8 %all-reduce.14.cloned.1.call-done = bf16[2048,768]{1,0:T(8,128)(2,1)} async-done(((bf16[2048,768]{1,0:T(8,128)(2,1)}), bf16[2048,768]{1,0:T(8,128)(2,1)}) %all-reduce.14.cloned.1.call-update) | async-done | bytes 3145744 | tf_op jit(solution)/shard_map/psum | solution.py:136
  128.2 4.1 fusion.74
  135.3 6.7 multiply_convert_fusion.1
  143.6 3.9 convolution_convert_fusion.3
  151.7 64.5 %all-reduce.16.cloned.1.call-done = bf16[2048,768]{1,0:T(8,128)(2,1)} async-done(((bf16[2048,768]{1,0:T(8,128)(2,1)}), bf16[2048,768]{1,0:T(8,128)(2,1)}) %all-reduce.16.cloned.1.call-update) | async-done | bytes 3145744 | tf_op jit(solution)/shard_map/psum | solution.py:148
  216.2 5.4 fusion.126
  227.2 4.7 fusion.125
  232.0 6.4 convert_reduce_fusion
  240.1 4.0 convolution_convert_fusion.2
  244.6 7.9 %fusion.114 = f32[768,768]{1,0:T(8,128)} fusion(bf16[2048,768]{1,0:T(8,128)(2,1)} %copy-done.48, f32[2048,768]{1,0:T(8,128)} %copy-done.7, f32[2048]{0:T(1024)} %copy-done.23), kind=kOutput, calls=%fused_computation.207 | convolution fusion | flops 2419064832 | bytes 11804672 | tf_op jit(solution)/shard_map/dot_general | solution.py:156
  256.0 8.6 %fusion.117 = f32[768,768]{1,0:T(8,128)} fusion(bf16[2048,768]{1,0:T(8,128)(2,1)} %copy-done.47, f32[768]{0:T(1024)S(1)} %copy-done.32, f32[768]{0:T(1024)S(1)} %get-tuple-element.346, f32[2048]{0:T(1024)S(1)} %copy-done.22, bf16[2048,768]{1,0:T(8,128)(2,1)} %all-reduce.14.cloned.1.call-done, bf16[2048,768]{1,0:T(8,128)(2,1)} %param.20, ...), kind=kOutput, calls=%fused_computation.210 | convolution fusion | flops 2430074880 | bytes 11822080 | tf_op jit(solution)/shard_map/dot_general | solution.py:160
  268.1 44.7 %all-reduce.18.cloned.1.call-done = bf16[2048,768]{1,0:T(8,128)(2,1)} async-done(((bf16[2048,768]{1,0:T(8,128)(2,1)}), bf16[2048,768]{1,0:T(8,128)(2,1)}) %all-reduce.18.cloned.1.call-update) | async-done | bytes 3145744 | tf_op jit(solution)/shard_map/psum | solution.py:166
  312.8 9.8 %multiply_reduce_fusion.2 = (f32[768]{0:T(1024)S(1)}, f32[2048]{0:T(1024)S(1)}, f32[768]{0:T(1024)S(1)}, f32[768]{0:T(1024)S(1)}) fusion(f32[2048]{0:T(1024)S(1)} %copy-done.22, bf16[2048,768]{1,0:T(8,128)(2,1)} %all-reduce.18.cloned.1.call-done, f32[2048,768]{1,0:T(8,128)} %copy-done.7, f32[2048]{0:T(1024)S(1)} %copy-done.24, ...), kind=kLoop, calls=%fused_computation.97 | loop fusion | flops 25161472 | bytes 15776768 | tf_op jit(solution)/shard_map/transpose(jvp())/reduce_sum | solution.py:31
  322.7 6.0 fusion.124
  337.7 43.6 %while.31 = (s32[]{:T(128)}, bf16[4,512,3,64]{1,3,2,0:T(8,128)(2,1)S(1)}, bf16[4,512,3,64]{1,3,2,0:T(8,128)(2,1)}, bf16[4,512,3,64]{1,3,2,0:T(8,128)(2,1)}, bf16...) while((s32[]{:T(128)}, ...), condition=%wide.region_23.24_spmd, body=%wide.region_19.23_spmd.sunk | while | flops 511226880 | bytes 26134740 | solution.py:174
  389.6 5.6 multiply_bitcast_fusion
  409.2 221.9 %all-reduce.20.cloned.1.call-done = (f32[8,55296]{1,0:T(8,128)}, f32[8,18432]{1,0:T(8,128)}, f32[8,73728]{1,0:T(8,128)}, f32[8,73728]{1,0:T(8,128)}) async-done(((f32[8,55296]{1,0:T(8,128)}, f32[8,18432]{1,0:T(8,128)}, f32[8,73728]{1,0:T(8,128)}, f32[8,73728]{1,0:T(8,128)}), (f32[8,55296]{1,0:T(8,128)}, f32[8,18432]{1,0:T(8,128)}, f32[8,73728]{1,0:T(8,128)}, ...) | async-done | bytes 7077904
  640.2 73.5 %all-gather.3.cloned.1.call-done = bf16[8192,768]{1,0:T(8,128)(2,1)} async-done(((bf16[2048,768]{1,0:T(8,128)(2,1)}), bf16[8192,768]{1,0:T(8,128)(2,1)}) %all-gather.3.cloned.1.call-update) | async-done | bytes 12582928 | tf_op jit(solution)/shard_map/all_gather | solution.py:195
  713.7 9.0 %reduce_sum.291 = bf16[2048,768]{1,0:T(8,128)(2,1)} reduce(bf16[4,2048,768]{2,1,0:T(8,128)(2,1)} %bitcast.210, bf16[]{:T(256)} %constant.248.clone.1), dimensions={0}, to_apply=%region_24.25 | reduce | flops 4718592 | bytes 15728642 | tf_op jit(solution)/shard_map/reduce_sum | solution.py:195
  722.7 6.0 add_reduce_fusion
  729.0 37.5 %all-reduce.7 = (f32[8,144]{1,0:T(8,128)S(1)}, f32[8,48]{1,0:T(8,128)S(1)}, f32[8,96]{1,0:T(8,128)S(1)}) all-reduce(f32[8,144]{1,0:T(8,128)S(1)} %reshape.865, f32[8,48]{1,0:T(8,128)S(1)} %reshape.871, f32[8,96]{1,0:T(8,128)S(1)} %reshape.872), channel_id=3, replica_groups=mesh['dp'=8,'mp'=4] {'dp'}, use_global_device_ids=true, to_apply=%region_31.32.clone | all-reduce | flops 2304 | bytes 18432
  769.3 9.2 %multiply_add_fusion.1 = (f32[1,1,221472]{2,1,0:T(1,128)}, f32[1,1,221472]{2,1,0:T(1,128)}, f32[1,1,221472]{2,1,0:T(1,128)}, f32[1,1,221472]{2,1,0:T(1,128)}) fusion(f32[1,1,221472]{2,1,0:T(1,128)S(1)} %copy-done.19, f32[1,1,221472]{2,1,0:T(1,128)} %param.31, f32[1,1,221472]{2,1,0:T(1,128)S(1)} %dynamic-update-slice.6, f32[1,1,221472]{2,1,0:T(1,128)} %param.32, ...), kind=kLoop, calls=%fused_computation.144 | loop fusion | flops 3986496 | bytes 7972992 | tf_op jit(solution)/shard_map/add | solution.py:224
  (296 shorter events, 151.2 us)
Async XLA Ops:
  7.2 128.1 %copy-start = (bf16[768,768]{1,0:T(8,128)(2,1)S(1)}, bf16[768,768]{1,0:T(8,128)(2,1)}, u32[]{:S(2)}) copy-start(bf16[768,768]{1,0:T(8,128)(2,1)} %param.25) | copy-start | bytes 3538948
  7.2 121.0 %all-reduce.14.cloned.1.call-start = ((), (), s32[]{:S(2)}) async-start(), calls=%async_computation | async-start | bytes 6291456 | tf_op jit(solution)/shard_map/psum | solution.py:136
  11.5 6.9 copy-start.40
  56.9 159.4 %all-reduce.16.cloned.1.call-start = ((), (), s32[]{:S(2)}) async-start(), calls=%async_computation.1 | async-start | bytes 6291456 | tf_op jit(solution)/shard_map/psum | solution.py:148
  128.2 7.1 copy-start.31
  128.2 7.1 copy-start.36
  135.2 6.7 copy-start.21
  135.3 8.3 %copy-start.41 = (bf16[768,768]{1,0:T(8,128)(2,1)S(1)}, bf16[768,768]{1,0:T(8,128)(2,1)}, u32[]{:S(2)}) copy-start(bf16[768,768]{1,0:T(8,128)(2,1)} %param.27) | copy-start | bytes 3538948
  147.5 165.3 %all-reduce.18.cloned.1.call-start = ((), (), s32[]{:S(2)}) async-start(), calls=%async_computation.2 | async-start | bytes 6291456 | tf_op jit(solution)/shard_map/psum | solution.py:166
  223.5 8.4 %slice-start = ((s8[6291456]{0:T(1024)(128)(4,1)}), s8[4194304]{0:T(1024)(128)(4,1)S(1)}, s32[]{:S(2)}) async-start(s8[6291456]{0:T(1024)(128)(4,1)} %bitcast.222), calls=%async_computation.5 | async-start | bytes 8388608
  232.0 6.4 copy-start.7
  244.1 11.9 %copy-start.22 = (f32[2048]{0:T(1024)S(1)}, f32[2048]{0:T(1024)}, u32[]{:S(2)}) copy-start(f32[2048]{0:T(1024)} %copy-done.21) | copy-start | bytes 24580
  244.1 11.9 %copy-start.32 = (f32[768]{0:T(1024)S(1)}, f32[768]{0:T(1024)}, u32[]{:S(2)}) copy-start(f32[768]{0:T(1024)} %get-tuple-element.345) | copy-start | bytes 9220
  244.1 387.1 %all-reduce.20.cloned.1.call-start = ((), (), s32[]{:S(2)}) async-start(), calls=%async_computation.4 | async-start | bytes 14155776
  256.0 56.8 %copy-start.24 = (f32[2048]{0:T(1024)S(1)}, f32[2048]{0:T(1024)}, u32[]{:S(2)}) copy-start(f32[2048]{0:T(1024)} %copy-done.23) | copy-start | bytes 24580
  268.1 54.5 %copy-start.27 = (f32[2048]{0:T(1024)S(1)}, f32[2048]{0:T(1024)}, u32[]{:S(2)}) copy-start(f32[2048]{0:T(1024)} %copy-done.26) | copy-start | bytes 24580
  312.8 9.8 %copy-start.4 = (bf16[2048,768]{1,0:T(8,128)(2,1)S(1)}, bf16[2048,768]{1,0:T(8,128)(2,1)}, u32[]{:S(2)}) copy-start(bf16[2048,768]{1,0:T(8,128)(2,1)} %param.20) | copy-start | bytes 9437188
  312.8 9.9 %copy-start.6 = (bf16[2048,768]{1,0:T(8,128)(2,1)S(1)}, bf16[2048,768]{1,0:T(8,128)(2,1)}, u32[]{:S(2)}) copy-start(bf16[2048,768]{1,0:T(8,128)(2,1)} %all-reduce.14.cloned.1.call-done) | copy-start | bytes 9437188
  312.8 9.9 %copy-start.8 = (bf16[2048,768]{1,0:T(8,128)(2,1)S(1)}, bf16[2048,768]{1,0:T(8,128)(2,1)}, u32[]{:S(2)}) copy-start(bf16[2048,768]{1,0:T(8,128)(2,1)} %all-reduce.18.cloned.1.call-done) | copy-start | bytes 9437188
  381.3 8.3 %copy-start.16 = (bf16[4,512,3,64]{1,3,2,0:T(8,128)(2,1)}, bf16[4,512,3,64]{1,3,2,0:T(8,128)(2,1)S(1)}, u32[]{:S(2)}) copy-start(bf16[4,512,3,64]{1,3,2,0:T(8,128)(2,1)S(1)} %get-tuple-element.256) | copy-start | bytes 2359300
  381.3 8.3 %copy-start.46 = (f32[3]{0:T(128)S(1)}, f32[3]{0:T(128)}, u32[]{:S(2)}) copy-start(f32[3]{0:T(128)} %constant.259.clone) | copy-start | bytes 40
  399.3 314.4 %all-gather.3.cloned.1.call-start = ((), (), s32[]{:S(2)}) async-start(), calls=%async_computation.3 | async-start | bytes 15728640 | tf_op jit(solution)/shard_map/all_gather | solution.py:195
  722.7 46.6 %copy-start.19 = (f32[1,1,221472]{2,1,0:T(1,128)S(1)}, f32[1,1,221472]{2,1,0:T(1,128)}, u32[]{:S(2)}) copy-start(f32[1,1,221472]{2,1,0:T(1,128)} %param.34) | copy-start | bytes 2657668
  722.7 55.7 %copy-start.1 = (bf16[768,768]{1,0:T(8,128)(2,1)S(1)}, bf16[768,768]{1,0:T(8,128)(2,1)}, u32[]{:S(2)}) copy-start(bf16[768,768]{1,0:T(8,128)(2,1)} %param.25) | copy-start | bytes 3538948
  (32 other events, 109.8 us)
Sparse Core Ops, SparseCore 0:
  57.0 71.1 all-reduce.13
  147.7 68.5 all-reduce.15
  244.2 68.5 all-reduce.17
  399.5 231.6 all-reduce.19
  632.6 81.1 all-gather.2
